TPU v7x, 128 devices: a whole 4x4x4 slice. The times are simulated.
128 devices in a mesh: bx: 16 (over x, z), by: 8 (over y, core).
Axes of the slice: x: 4, y: 4, z: 4, core: 2. Of those that a mesh axis runs over, the one named last changes fastest.
Arguments:
- features: bfloat16 [16, 8, 1024, 128], P('bx', 'by'), may hold values from -13 to 13
- live_count: int32 [16, 8], P('bx', 'by'), may hold values from 128 to 1024, as said below
- neighbour_map: int32 [16, 8, 27, 1024], P('bx', 'by'), may hold values from 0 to 2175, as said below
- send_rows: int32 [16, 8, 8, 128], P('bx', 'by'), may hold values from 0 to 1023, as said below
- weight: bfloat16 [3456, 128], replicated, may hold values from -0.109375 to 0.109375
- gain: float32 [128], replicated, may hold values from 0.5 to 1.5
- shift: float32 [128], replicated, may hold values from -3 to 3
- cotangent: bfloat16 [16, 8, 1024, 128], P('bx', 'by'), may hold values from -13 to 13
Outputs:
- activated: bfloat16 [16, 8, 1024, 128], P('bx', 'by')
- grad_features: bfloat16 [16, 8, 1024, 128], P('bx', 'by')
- grad_weight: float32 [27, 128, 128], P(None, 'bx', 'by')
Inputs may be any that keep to these rules, and one draw needn't show every extreme that they name: Rows 0 to live_count - 1 of a brick are live, the rest padding; in every draw some brick is full. `send_rows`: every entry is below its brick's live count; the eight blocks follow the directions (dx, dy) in row-major order with the brick's own position left out. `neighbour_map`: entries index the brick's extended table; offset 13 of a live row names that row itself; every entry of a padding row is 1536. With B = min(1024, 512) and q = r // B for a live row r, an entry below 1024 lies in rows q B to q B + B - 1, and an entry 1024 + b * 128 + h of incoming block b other than 4 has h in q * 128 B / 1024 to (q + 1) * 128 B / 1024 - 1.
All inputs are finite; a program needn't handle non-finite values.
Results may differ from a plain program's by a relative error of at most 0.029.
The roundings to bfloat16 on the way count: a program that leaves them out, or rounds other values in their place, can miss the bound.
Values may be sent and summed in bfloat16 or wider, within the bound.
No kernel may reach another device: no remote copies, remote signals or barrier semaphores. Data moves between devices by JAX's collectives and lax.ppermute only.
A program may use at most 64 MiB of HBM per device.

v0:
```python
import jax
import jax.numpy as jnp
from jax import lax
from jax.sharding import PartitionSpec as P

epsilon = 1e-05


def extended(cells, sides, width):
    for axis, dim in sides:
        count = lax.axis_size(axis)
        ends = count - 1
        head = lax.slice_in_dim(cells, 0, width, axis=dim)
        tail = lax.slice_in_dim(cells, cells.shape[dim] - width, cells.shape[dim], axis=dim)
        cells = jnp.concatenate(
            [
                lax.ppermute(tail, axis, [(i, (i + 1) % count) for i in range(ends)]),
                cells,
                lax.ppermute(head, axis, [((i + 1) % count, i) for i in range(ends)]),
            ],
            axis=dim,
        )
    return cells


def from_neighbours(outgoing):
    padded = extended(outgoing, (("bx", 0), ("by", 1)), 1)
    return padded[::2, ::2]


def per_device(features, live_count, neighbour_map, send_rows, weight, gain, shift, cotangent):
    own_rows = features[0, 0]
    rows_total, channels = own_rows.shape
    halo_rows = send_rows.shape[3]
    block_rows = min(rows_total, 512)
    blocks_count = rows_total // block_rows
    halo_window = halo_rows // blocks_count
    window_rows = block_rows + 9 * halo_window
    sent_index = send_rows[0, 0].reshape(-1)
    send_select = (
        sent_index[:, None] == lax.broadcasted_iota(jnp.int32, (1, rows_total), 1)
    ).astype(jnp.bfloat16)
    chosen_rows = jnp.dot(send_select, own_rows, preferred_element_type=jnp.float32).astype(
        jnp.bfloat16
    )
    chosen_rows = chosen_rows.reshape(8, halo_rows, channels)
    blank_block = jnp.zeros((1, halo_rows, channels), jnp.bfloat16)
    outgoing = jnp.concatenate([chosen_rows[:4], blank_block, chosen_rows[4:]], axis=0).reshape(
        3, 3, halo_rows, channels
    )
    incoming = from_neighbours(outgoing).reshape(9, blocks_count, halo_window, channels)
    index_blocks = neighbour_map[0, 0].reshape(27, blocks_count, block_rows).transpose(1, 0, 2)
    own_blocks = own_rows.reshape(blocks_count, block_rows, channels)
    halo_blocks = incoming.transpose(1, 0, 2, 3)
    block_ids = jnp.arange(blocks_count, dtype=jnp.int32)

    def selector_of(indices, block_index):
        beyond = indices - rows_total
        target = beyond // halo_rows
        inside = beyond - target * halo_rows - block_index * halo_window
        local_pos = indices - block_index * block_rows
        remote_pos = block_rows + target * halo_window + inside
        usable = (inside >= 0) & (inside < halo_window)
        position = jnp.where(indices < rows_total, local_pos, jnp.where(usable, remote_pos, -1))
        return position[:, :, None] == lax.broadcasted_iota(jnp.int32, (1, 1, window_rows), 2)

    def forward_block(pieces):
        indices, own_part, halo_part, block_index = pieces
        window = jnp.concatenate([own_part, halo_part.reshape(9 * halo_window, channels)], axis=0)
        selector = selector_of(indices, block_index).astype(jnp.bfloat16)
        gathered = jnp.einsum(
            "kbw,wc->bkc", selector, window, preferred_element_type=jnp.float32
        ).astype(jnp.bfloat16)
        columns = gathered.reshape(block_rows, 27 * channels)
        return (jnp.dot(columns, weight, preferred_element_type=jnp.float32), columns)

    conv_blocks, column_blocks = lax.map(
        forward_block, (index_blocks, own_blocks, halo_blocks, block_ids)
    )
    conv_out = conv_blocks.reshape(rows_total, channels).astype(jnp.bfloat16)
    conv_float = conv_out.astype(jnp.float32)
    live_mask = (lax.broadcasted_iota(jnp.int32, (rows_total, 1), 0) < live_count[0, 0]).astype(
        jnp.float32
    )
    local_count = jnp.sum(live_mask)
    total_sum, total_count = lax.psum(
        (jnp.sum(conv_float * live_mask, axis=0), local_count), ("bx", "by")
    )
    center = total_sum / total_count
    deviation = (conv_float - center) * live_mask
    variance = lax.psum(jnp.sum(deviation * deviation, axis=0), ("bx", "by")) / total_count
    inverse_std = lax.rsqrt(variance + epsilon)
    normalized = (conv_float - center) * inverse_std
    before = gain * normalized + shift
    activated = (jnp.maximum(before, 0.0) * live_mask).astype(jnp.bfloat16)
    upstream = cotangent[0, 0].astype(jnp.float32) * (before > 0.0) * live_mask
    sum_up, sum_cross = lax.psum(
        (jnp.sum(upstream, axis=0), jnp.sum(upstream * normalized, axis=0)), ("bx", "by")
    )
    conv_grad = (
        gain
        * inverse_std
        * (upstream - live_mask * (sum_up + normalized * sum_cross) / total_count)
    ).astype(jnp.bfloat16)
    grad_blocks = conv_grad.reshape(blocks_count, block_rows, channels)

    def backward_block(weight_acc, pieces):
        indices, columns, grad_rows, block_index = pieces
        weight_acc = weight_acc + lax.dot_general(
            columns, grad_rows, (((0,), (0,)), ((), ())), preferred_element_type=jnp.float32
        )
        column_grad = lax.dot_general(
            grad_rows, weight, (((1,), (1,)), ((), ())), preferred_element_type=jnp.float32
        )
        column_grad = column_grad.reshape(block_rows, 27, channels)
        selector = selector_of(indices, block_index).astype(jnp.float32)
        window_grad = jnp.einsum(
            "kbw,bkc->wc",
            selector,
            column_grad,
            precision=lax.Precision.HIGHEST,
            preferred_element_type=jnp.float32,
        )
        return (
            weight_acc,
            (window_grad[:block_rows], window_grad[block_rows:].reshape(9, halo_window, channels)),
        )

    start_acc = jnp.zeros((27 * channels, channels), jnp.float32)
    weight_acc, (own_parts, halo_parts) = lax.scan(
        backward_block, start_acc, (index_blocks, column_blocks, grad_blocks, block_ids)
    )
    weight_terms = weight_acc.reshape(27, channels, channels)
    partial_x = lax.psum_scatter(
        weight_terms.astype(jnp.bfloat16), "bx", scatter_dimension=1, tiled=True
    )
    summed = lax.psum_scatter(partial_x, "by", scatter_dimension=2, tiled=True).astype(jnp.float32)
    grad_weight = summed / jnp.sqrt(total_count)
    own_table = own_parts.reshape(rows_total, channels)
    halo_table = halo_parts.transpose(1, 0, 2, 3).reshape(3, 3, halo_rows, channels)
    halo_grad = halo_table.astype(jnp.bfloat16)
    returned = from_neighbours(halo_grad).reshape(9, halo_rows, channels)
    slots_back = (
        jnp.concatenate([returned[:4], returned[5:]], axis=0)
        .reshape(-1, channels)
        .astype(jnp.float32)
    )
    added_back = lax.dot_general(
        send_select.astype(jnp.float32),
        slots_back,
        (((0,), (0,)), ((), ())),
        precision=lax.Precision.HIGHEST,
        preferred_element_type=jnp.float32,
    )
    own_grad = own_table + added_back
    return (activated[None, None], own_grad.astype(jnp.bfloat16)[None, None], grad_weight)


def solution(mesh):
    return jax.shard_map(
        per_device,
        mesh=mesh,
        in_specs=(
            P("bx", "by", None, None),
            P("bx", "by"),
            P("bx", "by", None, None),
            P("bx", "by", None, None),
            P(),
            P(),
            P(),
            P("bx", "by", None, None),
        ),
        out_specs=(P("bx", "by", None, None), P("bx", "by", None, None), P(None, "bx", "by")),
        check_vma=False,
    )
```

profile of v0, /device:TPU:0, one launch (start us, length us, event | category | flops | bytes accessed | tf_op | source)
XLA Modules:
  0.0 465.1 jit_solution(409183118276341036)
XLA Ops:
  7.2 1.9 fusion.34
  9.1 3.9 collective-permute-start
  13.0 1.3 collective-permute-start.1
  15.2 4.3 collective-permute-done.1
  19.5 0.8 pad_maximum_fusion.9
  20.3 1.9 collective-permute-start.2
  22.2 1.3 collective-permute-start.3
  23.6 1.2 reduce.4
  25.5 1.5 collective-permute-done.3
  27.0 1.1 pad_maximum_fusion
  28.2 38.2 %while.33 = (s32[]{:T(128)}, bf16[2,512,128]{2,1,0:T(8,128)(2,1)S(1)}, bf16[2,512,3456]{1,2,0:T(8,128)(2,1)}, bf16[2,512,128]{2,1,0:T(8,128)(2,1)}, bf16[2,9,64,...) while((s32[]{:T(128)}, ...), condition=%wide.region_1.2_spmd.clone, body=%wide.region_0.1_spmd.sunk.clone | while | flops 4321123840 | bytes 16304801 | solution.py:77
  30.2 0.9 dynamic-slice_bitcast_fusion.3
  31.2 13.0 %fusion.82 = bf16[128,27,512]{2,0,1:T(8,128)(2,1)S(1)} fusion(s32[27,512]{1,0:T(8,128)S(1)} %bitcast_select_fusion.6, bf16[576,128]{1,0:T(8,128)(2,1)S(1)} %bitcast.223, bf16[512,128]{1,0:T(8,128)(2,1)S(1)} %dynamic-slice_bitcast_fusion.3), kind=kOutput, calls=%fused_computation.3.clone.1.clone | convolution fusion | flops 3867738112 | bytes 3872768 | tf_op jit(solution)/shard_map/while/body/eval_jaxpr/kbw,wc->bkc/dot_general | solution.py:71
  44.1 2.0 constant_dynamic-update-slice_fusion.6
  46.1 1.2 fusion.83
  49.3 0.9 dynamic-slice_bitcast_fusion.3
  50.2 13.0 %fusion.82 = bf16[128,27,512]{2,0,1:T(8,128)(2,1)S(1)} fusion(s32[27,512]{1,0:T(8,128)S(1)} %bitcast_select_fusion.6, bf16[576,128]{1,0:T(8,128)(2,1)S(1)} %bitcast.223, bf16[512,128]{1,0:T(8,128)(2,1)S(1)} %dynamic-slice_bitcast_fusion.3), kind=kOutput, calls=%fused_computation.3.clone.1.clone | convolution fusion | flops 3867738112 | bytes 3872768 | tf_op jit(solution)/shard_map/while/body/eval_jaxpr/kbw,wc->bkc/dot_general | solution.py:71
  63.2 2.0 constant_dynamic-update-slice_fusion.6
  65.2 1.2 fusion.83
  66.6 70.3 %all-reduce.2 = (f32[128]{0:T(128)S(1)}, f32[]{:T(128)}) all-reduce(f32[128]{0:T(128)S(1)} %multiply_reduce_fusion.1, f32[]{:T(128)} %fusion.44), channel_id=1, replica_groups=mesh['bx'=16,'by'=8] {'bx','by'}, use_global_device_ids=true, to_apply=%region_3.4 | all-reduce | flops 129 | bytes 1032 | tf_op jit(solution)/shard_map/psum | solution.py:86
  137.8 62.7 %psum.37 = f32[128]{0:T(128)S(1)} all-reduce(f32[128]{0:T(128)S(1)} %multiply_reduce_fusion), channel_id=1, replica_groups=mesh['bx'=16,'by'=8] {'bx','by'}, use_global_device_ids=true, to_apply=%region_7.8 | all-reduce | flops 128 | bytes 1024 | tf_op jit(solution)/shard_map/psum | solution.py:91
  201.2 1.2 fusion.39
  202.4 64.2 %all-reduce.1 = (f32[128]{0:T(128)S(1)}, f32[128]{0:T(128)S(1)}) all-reduce(f32[128]{0:T(128)S(1)} %get-tuple-element.329, f32[128]{0:T(128)S(1)} %get-tuple-element.328), channel_id=1, replica_groups=mesh['bx'=16,'by'=8] {'bx','by'}, use_global_device_ids=true, to_apply=%region_11.12 | all-reduce | flops 256 | bytes 2048 | tf_op jit(solution)/shard_map/psum | solution.py:97
  266.6 1.9 fusion.42
  268.5 73.1 %while.34 = (s32[]{:T(128)}, f32[3456,128]{1,0:T(8,128)S(1)}, f32[2,512,128]{2,1,0:T(8,128)}, bf16[2,9,64,128]{3,2,0,1:T(8,128)(2,1)}, bf16[2,512,3456]{1,2,0:T(...) while((s32[]{:T(128)}, f32[3456,128]{1,0:T(8,128)S(1)}, ...), condition=%wide.region_13.14_spmd.clone.clone, body=%wide.region_12.13_spmd.clone.sunk.clone | while | flops 24024522752 | bytes 28413672 | solution.py:130
  270.5 1.1 fusion.89
  271.6 28.7 %fusion.90 = f32[1088,128]{1,0:T(8,128)S(1)} fusion(f32[512,27,128]{2,0,1:T(8,128)S(1)} %fusion.89, s32[27,512]{1,0:T(8,128)S(1)} %bitcast_select_fusion.7), kind=kOutput, calls=%fused_computation.31.clone.1.clone | convolution fusion | flops 23117266944 | bytes 7690240 | tf_op jit(solution)/shard_map/while/body/eval_jaxpr/kbw,bkc->wc/dot_general | solution.py:117
  301.8 3.2 convolution_add_fusion.3
  307.1 1.1 fusion.89
  308.2 28.7 %fusion.90 = f32[1088,128]{1,0:T(8,128)S(1)} fusion(f32[512,27,128]{2,0,1:T(8,128)S(1)} %fusion.89, s32[27,512]{1,0:T(8,128)S(1)} %bitcast_select_fusion.7), kind=kOutput, calls=%fused_computation.31.clone.1.clone | convolution fusion | flops 23117266944 | bytes 7690240 | tf_op jit(solution)/shard_map/while/body/eval_jaxpr/kbw,bkc->wc/dot_general | solution.py:117
  338.4 3.2 convolution_add_fusion.3
  341.7 1.0 convert_element_type.131
  342.8 1.0 fusion.48
  343.7 1.3 collective-permute-start.4
  345.0 1.3 collective-permute-start.5
  348.3 4.0 collective-permute-done.5
  352.3 1.0 pad_maximum_fusion.6
  353.3 1.5 collective-permute-start.6
  354.8 1.3 collective-permute-start.7
  356.1 0.9 multiply_convert_fusion
  357.1 2.2 collective-permute-done.7
  359.3 1.1 pad_maximum_fusion.1
  360.5 64.4 %all-reduce.5.cloned.1.call-done = bf16[27,128,128]{2,1,0:T(8,128)(2,1)} async-done(((bf16[27,128,128]{2,1,0:T(8,128)(2,1)}), bf16[27,128,128]{2,1,0:T(8,128)(2,1)}) %all-reduce.5.cloned.1.call-update) | async-done | bytes 884752
  424.9 0.8 constant_dynamic-slice_fusion.1
  425.7 0.9 copy.30
  426.7 3.2 fusion.35
  429.9 27.0 %reduce-scatter.3.cloned.1.call-done = bf16[27,8,16]{0,1,2:T(8,128)(2,1)} async-done(((bf16[27,8,128]{0,1,2:T(8,128)(2,1)}), bf16[27,8,16]{0,1,2:T(8,128)(2,1)}) %reduce-scatter.3.cloned.1.call-update) | async-done | bytes 6928 | tf_op jit(solution)/shard_map/reduce_scatter | solution.py:137
  456.9 0.8 convert_divide_fusion
  (68 shorter events, 9.9 us)
Async XLA Ops:
  7.2 21.0 %copy-start = (bf16[3456,128]{1,0:T(8,128)(2,1)S(1)}, bf16[3456,128]{1,0:T(8,128)(2,1)}, u32[]{:S(2)}) copy-start(bf16[3456,128]{1,0:T(8,128)(2,1)} %param.16) | copy-start | bytes 2654212
  7.2 417.8 %all-reduce.5.cloned.1.call-start = ((), (), s32[]{:S(2)}) async-start(), calls=%async_computation.2 | async-start | bytes 1769472
  9.1 6.1 %collective-permute-start = (bf16[1,3,128,128]{3,2,1,0:T(8,128)(2,1)S(1)}, bf16[1,3,128,128]{3,2,1,0:T(8,128)(2,1)S(1)}, u32[]{:S(2)}, u32[]{:S(2)}) collective-permute-start(bf16[1,3,128,128]{3,2,1,0:T(8,128)(2,1)S(1)} %bitcast.239), channel_id=1, source_target_pairs={{0,8},{8,16},{16,24},{24,32},{32,40},{40,48},{48,56},{56,64},{64,7... | collective-permute-start | bytes 294920 | tf_op jit(solution)/shard_map/ppermute | solution.py:17
  13.0 6.5 %collective-permute-start.1 = (bf16[1,3,128,128]{3,2,1,0:T(8,128)(2,1)S(1)}, bf16[1,3,128,128]{3,2,1,0:T(8,128)(2,1)S(1)}, u32[]{:S(2)}, u32[]{:S(2)}) collective-permute-start(bf16[1,3,128,128]{3,2,1,0:T(8,128)(2,1)S(1)} %bitcast.238), channel_id=1, source_target_pairs={{8,0},{16,8},{24,16},{32,24},{40,32},{48,40},{56,48},{64,56},{72,6... | collective-permute-start | bytes 294920 | tf_op jit(solution)/shard_map/ppermute | solution.py:19
  20.3 5.2 %collective-permute-start.2 = (bf16[5,1,128,128]{3,2,1,0:T(8,128)(2,1)}, bf16[5,1,128,128]{3,2,1,0:T(8,128)(2,1)}, u32[]{:S(2)}, u32[]{:S(2)}) collective-permute-start(bf16[5,1,128,128]{3,2,1,0:T(8,128)(2,1)} %get-tuple-element.372), channel_id=1, source_target_pairs={{0,1},{1,2},{2,3},{3,4},{4,5},{5,6},{6,7},{8,9},{9,10},{10,11},{11... | collective-permute-start | bytes 491528 | tf_op jit(solution)/shard_map/ppermute | solution.py:17
  22.2 4.8 %collective-permute-start.3 = (bf16[5,1,128,128]{3,2,1,0:T(8,128)(2,1)}, bf16[5,1,128,128]{3,2,1,0:T(8,128)(2,1)}, u32[]{:S(2)}, u32[]{:S(2)}) collective-permute-start(bf16[5,1,128,128]{3,2,1,0:T(8,128)(2,1)} %get-tuple-element.373), channel_id=1, source_target_pairs={{1,0},{2,1},{3,2},{4,3},{5,4},{6,5},{7,6},{9,8},{10,9},{11,10},{12... | collective-permute-start | bytes 491528 | tf_op jit(solution)/shard_map/ppermute | solution.py:19
  28.2 172.3 %copy-start.1 = (f32[128]{0:T(128)S(1)}, f32[128]{0:T(128)}, u32[]{:S(2)}) copy-start(f32[128]{0:T(128)} %param.17) | copy-start | bytes 1540
  28.2 173.0 %copy-start.2 = (f32[128]{0:T(128)S(1)}, f32[128]{0:T(128)}, u32[]{:S(2)}) copy-start(f32[128]{0:T(128)} %param.18) | copy-start | bytes 1540
  268.5 77.9 %copy-start.6 = (u32[128]{0:T(128)S(1)}, u32[128]{0:T(128)}, u32[]{:S(2)}) copy-start(u32[128]{0:T(128)} %constant.182) | copy-start | bytes 1540
  271.6 28.7 %copy-start.3 = (f32[2,512,128]{2,1,0:T(8,128)S(1)}, f32[2,512,128]{2,1,0:T(8,128)}, u32[]{:S(2)}) copy-start(f32[2,512,128]{2,1,0:T(8,128)} %get-tuple-element.580) | copy-start | bytes 1572868 | tf_op jit(solution)/shard_map/while
  300.4 0.8 copy-start.4
  308.1 28.7 %copy-start.3 = (f32[2,512,128]{2,1,0:T(8,128)S(1)}, f32[2,512,128]{2,1,0:T(8,128)}, u32[]{:S(2)}) copy-start(f32[2,512,128]{2,1,0:T(8,128)} %get-tuple-element.580) | copy-start | bytes 1572868 | tf_op jit(solution)/shard_map/while
  336.9 0.8 copy-start.4
  341.6 85.0 %copy-start.5 = (s32[1,1,8,128]{3,2,1,0:T(8,128)S(1)}, s32[1,1,8,128]{3,2,1,0:T(8,128)}, u32[]{:S(2)}) copy-start(s32[1,1,8,128]{3,2,1,0:T(8,128)} %param.15) | copy-start | bytes 12292
  342.7 114.2 %reduce-scatter.3.cloned.1.call-start = ((), (), s32[]{:S(2)}) async-start(), calls=%async_computation.1 | async-start | bytes 294912 | tf_op jit(solution)/shard_map/reduce_scatter | solution.py:137
  343.7 4.6 collective-permute-start.4
  345.0 7.3 %collective-permute-start.5 = (bf16[1,3,128,128]{3,2,1,0:T(8,128)(2,1)S(1)}, bf16[1,3,128,128]{3,2,1,0:T(8,128)(2,1)S(1)}, u32[]{:S(2)}, u32[]{:S(2)}) collective-permute-start(bf16[1,3,128,128]{3,2,1,0:T(8,128)(2,1)S(1)} %bitcast.236), channel_id=1, source_target_pairs={{8,0},{16,8},{24,16},{32,24},{40,32},{48,40},{56,48},{64,56},{72,6... | collective-permute-start | bytes 294920 | tf_op jit(solution)/shard_map/ppermute | solution.py:19
  353.3 3.7 collective-permute-start.6
  354.8 4.5 collective-permute-start.7
Sparse Core Ops, SparseCore 0:
  342.8 82.0 all-reduce.4
  427.3 29.5 reduce-scatter.2
where the time goes:
time: 466 us; the launch traced here: 465 us
  blocking collectives  197 us (42%)
  waiting for transfers between devices  104 us (22%)
  matrix products  99.4 us (21%)
  between operations  16.4 us (4%)
  local copies, waits for them, and re-layouts  15.4 us (3%)
  starting transfers between devices  13.9 us (3%)
  other arithmetic  13.7 us (3%)
  loops' own time  5.44 us (1%)
    psum x1, blocking collectives, per_device(): lax.psum((jnp.sum(conv_float * live_mask, axis=0), local_count), ('bx', '...  70.3 us
    unnamed x3, waiting for transfers between devices  64.5 us
    psum x1, blocking collectives, per_device(): lax.psum((jnp.sum(upstream, axis=0), jnp.sum(upstream * normalized, axis=...  64.2 us
    psum x1, blocking collectives, per_device(): lax.psum(jnp.sum(deviation * deviation, axis=0), ('bx', 'by')) / total_count  62.7 us
    dot_general x2, matrix products, backward_block(): jnp.einsum('kbw,bkc->wc', selector, column_grad, precision=lax.Precision....  57.4 us
    reduce_scatter x1, waiting for transfers between devices, per_device(): lax.psum_scatter(partial_x, 'by', scatter_dimension=2, tiled=True)  27 us
    dot_general x2, matrix products, forward_block(): jnp.einsum('kbw,wc->bkc', selector, window, preferred_element_type=jnp.fl...  25.9 us
    ppermute x4, waiting for transfers between devices, extended(): lax.ppermute(head, axis, [((i + 1) % count, i) for i in range(ends)])  12.1 us
  transfers between devices with their start and end apart: 10, of which 6 were waited for; matrix products, arithmetic and copies ran while one was open for 2% of the time, Pallas kernels for 0%

commit v1 on v0

--- a/solution.py
+++ b/solution.py
@@ -4,6 +4,7 @@
 from jax.sharding import PartitionSpec as P
 
 epsilon = 1e-05
+read_values = lambda content: lax.psum(lax.psum(content, "bx"), "by")
 
 
 def extended(cells, sides, width):
@@ -94,8 +95,8 @@
     before = gain * normalized + shift
     activated = (jnp.maximum(before, 0.0) * live_mask).astype(jnp.bfloat16)
     upstream = cotangent[0, 0].astype(jnp.float32) * (before > 0.0) * live_mask
-    sum_up, sum_cross = lax.psum(
-        (jnp.sum(upstream, axis=0), jnp.sum(upstream * normalized, axis=0)), ("bx", "by")
+    sum_up, sum_cross = read_values(
+        (jnp.sum(upstream, axis=0), jnp.sum(upstream * normalized, axis=0))
     )
     conv_grad = (
         gain

time: 466 us -> 450 us (0.966)
  blocking collectives: 197 us -> 184 us
    psum x1 -> x2, blocking collectives: 64.2 us -> 50.7 us  [read_values = lambda content: lax.psum(lax.psum(content, 'bx'), 'by')]
where the time goes in v1:
time: 450 us; the launch traced here: 449 us
  blocking collectives  184 us (41%)
  waiting for transfers between devices  101 us (22%)
  matrix products  99.4 us (22%)
  between operations  16.4 us (4%)
  local copies, waits for them, and re-layouts  15.5 us (3%)
  starting transfers between devices  13.7 us (3%)
  other arithmetic  13.7 us (3%)
  loops' own time  5.44 us (1%)
    psum x1, blocking collectives, per_device(): lax.psum((jnp.sum(conv_float * live_mask, axis=0), local_count), ('bx', '...  70.3 us
    unnamed x3, waiting for transfers between devices  62.7 us
    psum x1, blocking collectives, per_device(): lax.psum(jnp.sum(deviation * deviation, axis=0), ('bx', 'by')) / total_count  62.7 us
    dot_general x2, matrix products, backward_block(): jnp.einsum('kbw,bkc->wc', selector, column_grad, precision=lax.Precision....  57.4 us
    psum x2, blocking collectives, read_values = lambda content: lax.psum(lax.psum(content, 'bx'), 'by')  50.7 us
    reduce_scatter x1, waiting for transfers between devices, per_device(): lax.psum_scatter(partial_x, 'by', scatter_dimension=2, tiled=True)  27 us
    dot_general x2, matrix products, forward_block(): jnp.einsum('kbw,wc->bkc', selector, window, preferred_element_type=jnp.fl...  25.9 us
    ppermute x4, waiting for transfers between devices, extended(): lax.ppermute(head, axis, [((i + 1) % count, i) for i in range(ends)])  11.4 us
  transfers between devices with their start and end apart: 10, of which 6 were waited for; matrix products, arithmetic and copies ran while one was open for 2% of the time, Pallas kernels for 0%

profile of v1, /device:TPU:0, one launch (start us, length us, event | category | flops | bytes accessed | tf_op | source)
XLA Modules:
  0.0 448.9 jit_solution(15977965210708864169)
XLA Ops:
  7.2 1.9 fusion.34
  9.1 3.9 collective-permute-start
  13.0 1.3 collective-permute-start.1
  15.2 4.3 collective-permute-done.1
  20.3 1.9 collective-permute-start.2
  22.2 1.3 collective-permute-start.3
  23.6 1.2 reduce.4
  25.5 1.5 collective-permute-done.3
  27.0 1.1 pad_maximum_fusion
  28.2 38.2 %while.33 = (s32[]{:T(128)}, bf16[2,512,128]{2,1,0:T(8,128)(2,1)S(1)}, bf16[2,512,3456]{1,2,0:T(8,128)(2,1)}, bf16[2,512,128]{2,1,0:T(8,128)(2,1)}, bf16[2,9,64,...) while((s32[]{:T(128)}, ...), condition=%wide.region_1.2_spmd.clone, body=%wide.region_0.1_spmd.sunk.clone | while | flops 4321123840 | bytes 16304801 | solution.py:78
  30.2 0.9 dynamic-slice_bitcast_fusion.3
  31.2 13.0 %fusion.82 = bf16[128,27,512]{2,0,1:T(8,128)(2,1)S(1)} fusion(s32[27,512]{1,0:T(8,128)S(1)} %bitcast_select_fusion.6, bf16[576,128]{1,0:T(8,128)(2,1)S(1)} %bitcast.223, bf16[512,128]{1,0:T(8,128)(2,1)S(1)} %dynamic-slice_bitcast_fusion.3), kind=kOutput, calls=%fused_computation.3.clone.1.clone | convolution fusion | flops 3867738112 | bytes 3872768 | tf_op jit(solution)/shard_map/while/body/eval_jaxpr/kbw,wc->bkc/dot_general | solution.py:72
  44.1 2.0 constant_dynamic-update-slice_fusion.6
  46.1 1.2 fusion.83
  49.3 0.9 dynamic-slice_bitcast_fusion.3
  50.2 13.0 %fusion.82 = bf16[128,27,512]{2,0,1:T(8,128)(2,1)S(1)} fusion(s32[27,512]{1,0:T(8,128)S(1)} %bitcast_select_fusion.6, bf16[576,128]{1,0:T(8,128)(2,1)S(1)} %bitcast.223, bf16[512,128]{1,0:T(8,128)(2,1)S(1)} %dynamic-slice_bitcast_fusion.3), kind=kOutput, calls=%fused_computation.3.clone.1.clone | convolution fusion | flops 3867738112 | bytes 3872768 | tf_op jit(solution)/shard_map/while/body/eval_jaxpr/kbw,wc->bkc/dot_general | solution.py:72
  63.2 2.0 constant_dynamic-update-slice_fusion.6
  65.3 1.2 fusion.83
  66.7 70.3 %all-reduce.1 = (f32[128]{0:T(128)S(1)}, f32[]{:T(128)}) all-reduce(f32[128]{0:T(128)S(1)} %multiply_reduce_fusion.1, f32[]{:T(128)} %fusion.44), channel_id=1, replica_groups=mesh['bx'=16,'by'=8] {'bx','by'}, use_global_device_ids=true, to_apply=%region_3.4 | all-reduce | flops 129 | bytes 1032 | tf_op jit(solution)/shard_map/psum | solution.py:87
  137.8 62.7 %psum.51 = f32[128]{0:T(128)S(1)} all-reduce(f32[128]{0:T(128)S(1)} %multiply_reduce_fusion), channel_id=1, replica_groups=mesh['bx'=16,'by'=8] {'bx','by'}, use_global_device_ids=true, to_apply=%region_7.8 | all-reduce | flops 128 | bytes 1024 | tf_op jit(solution)/shard_map/psum | solution.py:92
  201.2 1.2 fusion.39
  202.4 38.1 %all-reduce.2 = (f32[128]{0:T(128)S(1)}, f32[128]{0:T(128)S(1)}) all-reduce(f32[128]{0:T(128)S(1)} %get-tuple-element.329, f32[128]{0:T(128)S(1)} %get-tuple-element.328), channel_id=1, replica_groups=mesh['bx'=16,'by'=8] {'bx'}, use_global_device_ids=true, to_apply=%region_12.13 | all-reduce | flops 256 | bytes 2048 | tf_op jit(solution)/shard_map/psum | solution.py:7
  240.5 12.6 %all-reduce.3 = (f32[128]{0:T(128)S(1)}, f32[128]{0:T(128)S(1)}) all-reduce(f32[128]{0:T(128)S(1)} %get-tuple-element.366, f32[128]{0:T(128)S(1)} %get-tuple-element.367), channel_id=1, replica_groups=mesh['bx'=16,'by'=8] {'by'}, use_global_device_ids=true, to_apply=%region_13.14 | all-reduce | flops 256 | bytes 2048 | tf_op jit(solution)/shard_map/psum | solution.py:7
  253.1 1.9 fusion.42
  255.0 73.2 %while.34 = (s32[]{:T(128)}, f32[3456,128]{1,0:T(8,128)S(1)}, f32[2,512,128]{2,1,0:T(8,128)}, bf16[2,9,64,128]{3,2,0,1:T(8,128)(2,1)}, bf16[2,512,3456]{1,2,0:T(...) while((s32[]{:T(128)}, f32[3456,128]{1,0:T(8,128)S(1)}, ...), condition=%wide.region_15.16_spmd.clone.clone, body=%wide.region_14.15_spmd.clone.sunk.clone | while | flops 24024522752 | bytes 28413672 | solution.py:131
  256.9 1.1 fusion.89
  258.0 28.7 %fusion.90 = f32[1088,128]{1,0:T(8,128)S(1)} fusion(f32[512,27,128]{2,0,1:T(8,128)S(1)} %fusion.89, s32[27,512]{1,0:T(8,128)S(1)} %bitcast_select_fusion.7), kind=kOutput, calls=%fused_computation.31.clone.1.clone | convolution fusion | flops 23117266944 | bytes 7690240 | tf_op jit(solution)/shard_map/while/body/eval_jaxpr/kbw,bkc->wc/dot_general | solution.py:118
  288.3 3.2 convolution_add_fusion.3
  293.5 1.1 fusion.89
  294.6 28.7 %fusion.90 = f32[1088,128]{1,0:T(8,128)S(1)} fusion(f32[512,27,128]{2,0,1:T(8,128)S(1)} %fusion.89, s32[27,512]{1,0:T(8,128)S(1)} %bitcast_select_fusion.7), kind=kOutput, calls=%fused_computation.31.clone.1.clone | convolution fusion | flops 23117266944 | bytes 7690240 | tf_op jit(solution)/shard_map/while/body/eval_jaxpr/kbw,bkc->wc/dot_general | solution.py:118
  324.9 3.2 convolution_add_fusion.3
  328.1 1.0 convert_element_type.131
  329.2 1.0 fusion.48
  330.2 1.3 collective-permute-start.4
  331.5 1.3 collective-permute-start.5
  334.8 4.4 collective-permute-done.5
  339.2 1.0 pad_maximum_fusion.6
  340.2 1.3 collective-permute-start.6
  341.5 1.3 collective-permute-start.7
  342.8 0.9 multiply_convert_fusion
  343.7 1.1 collective-permute-done.7
  344.8 1.1 pad_maximum_fusion.1
  346.0 62.7 %all-reduce.6.cloned.1.call-done = bf16[27,128,128]{2,1,0:T(8,128)(2,1)} async-done(((bf16[27,128,128]{2,1,0:T(8,128)(2,1)}), bf16[27,128,128]{2,1,0:T(8,128)(2,1)}) %all-reduce.6.cloned.1.call-update) | async-done | bytes 884752
  408.7 0.8 constant_dynamic-slice_fusion.1
  409.5 0.9 copy.30
  410.4 3.2 fusion.35
  413.6 27.0 %reduce-scatter.3.cloned.1.call-done = bf16[27,8,16]{0,1,2:T(8,128)(2,1)} async-done(((bf16[27,8,128]{0,1,2:T(8,128)(2,1)}), bf16[27,8,16]{0,1,2:T(8,128)(2,1)}) %reduce-scatter.3.cloned.1.call-update) | async-done | bytes 6928 | tf_op jit(solution)/shard_map/reduce_scatter | solution.py:138
  440.6 0.8 convert_divide_fusion
  (69 shorter events, 10.6 us)
Async XLA Ops:
  7.2 21.0 %copy-start = (bf16[3456,128]{1,0:T(8,128)(2,1)S(1)}, bf16[3456,128]{1,0:T(8,128)(2,1)}, u32[]{:S(2)}) copy-start(bf16[3456,128]{1,0:T(8,128)(2,1)} %param.16) | copy-start | bytes 2654212
  7.2 401.5 %all-reduce.6.cloned.1.call-start = ((), (), s32[]{:S(2)}) async-start(), calls=%async_computation.2 | async-start | bytes 1769472
  9.1 6.1 %collective-permute-start = (bf16[1,3,128,128]{3,2,1,0:T(8,128)(2,1)S(1)}, bf16[1,3,128,128]{3,2,1,0:T(8,128)(2,1)S(1)}, u32[]{:S(2)}, u32[]{:S(2)}) collective-permute-start(bf16[1,3,128,128]{3,2,1,0:T(8,128)(2,1)S(1)} %bitcast.239), channel_id=1, source_target_pairs={{0,8},{8,16},{16,24},{24,32},{32,40},{40,48},{48,56},{56,64},{64,7... | collective-permute-start | bytes 294920 | tf_op jit(solution)/shard_map/ppermute | solution.py:18
  13.0 6.5 %collective-permute-start.1 = (bf16[1,3,128,128]{3,2,1,0:T(8,128)(2,1)S(1)}, bf16[1,3,128,128]{3,2,1,0:T(8,128)(2,1)S(1)}, u32[]{:S(2)}, u32[]{:S(2)}) collective-permute-start(bf16[1,3,128,128]{3,2,1,0:T(8,128)(2,1)S(1)} %bitcast.238), channel_id=1, source_target_pairs={{8,0},{16,8},{24,16},{32,24},{40,32},{48,40},{56,48},{64,56},{72,6... | collective-permute-start | bytes 294920 | tf_op jit(solution)/shard_map/ppermute | solution.py:20
  20.3 5.2 %collective-permute-start.2 = (bf16[5,1,128,128]{3,2,1,0:T(8,128)(2,1)}, bf16[5,1,128,128]{3,2,1,0:T(8,128)(2,1)}, u32[]{:S(2)}, u32[]{:S(2)}) collective-permute-start(bf16[5,1,128,128]{3,2,1,0:T(8,128)(2,1)} %get-tuple-element.374), channel_id=1, source_target_pairs={{0,1},{1,2},{2,3},{3,4},{4,5},{5,6},{6,7},{8,9},{9,10},{10,11},{11... | collective-permute-start | bytes 491528 | tf_op jit(solution)/shard_map/ppermute | solution.py:18
  22.2 4.8 %collective-permute-start.3 = (bf16[5,1,128,128]{3,2,1,0:T(8,128)(2,1)}, bf16[5,1,128,128]{3,2,1,0:T(8,128)(2,1)}, u32[]{:S(2)}, u32[]{:S(2)}) collective-permute-start(bf16[5,1,128,128]{3,2,1,0:T(8,128)(2,1)} %get-tuple-element.375), channel_id=1, source_target_pairs={{1,0},{2,1},{3,2},{4,3},{5,4},{6,5},{7,6},{9,8},{10,9},{11,10},{12... | collective-permute-start | bytes 491528 | tf_op jit(solution)/shard_map/ppermute | solution.py:20
  28.2 172.3 %copy-start.1 = (f32[128]{0:T(128)S(1)}, f32[128]{0:T(128)}, u32[]{:S(2)}) copy-start(f32[128]{0:T(128)} %param.17) | copy-start | bytes 1540
  28.2 173.0 %copy-start.2 = (f32[128]{0:T(128)S(1)}, f32[128]{0:T(128)}, u32[]{:S(2)}) copy-start(f32[128]{0:T(128)} %param.18) | copy-start | bytes 1540
  254.9 77.9 %copy-start.6 = (u32[128]{0:T(128)S(1)}, u32[128]{0:T(128)}, u32[]{:S(2)}) copy-start(u32[128]{0:T(128)} %constant.182) | copy-start | bytes 1540
  258.0 28.7 %copy-start.3 = (f32[2,512,128]{2,1,0:T(8,128)S(1)}, f32[2,512,128]{2,1,0:T(8,128)}, u32[]{:S(2)}) copy-start(f32[2,512,128]{2,1,0:T(8,128)} %get-tuple-element.582) | copy-start | bytes 1572868 | tf_op jit(solution)/shard_map/while
  286.8 0.8 copy-start.4
  294.6 28.7 %copy-start.3 = (f32[2,512,128]{2,1,0:T(8,128)S(1)}, f32[2,512,128]{2,1,0:T(8,128)}, u32[]{:S(2)}) copy-start(f32[2,512,128]{2,1,0:T(8,128)} %get-tuple-element.582) | copy-start | bytes 1572868 | tf_op jit(solution)/shard_map/while
  323.4 0.8 copy-start.4
  328.1 82.3 %copy-start.5 = (s32[1,1,8,128]{3,2,1,0:T(8,128)S(1)}, s32[1,1,8,128]{3,2,1,0:T(8,128)}, u32[]{:S(2)}) copy-start(s32[1,1,8,128]{3,2,1,0:T(8,128)} %param.15) | copy-start | bytes 12292
  329.2 111.4 %reduce-scatter.3.cloned.1.call-start = ((), (), s32[]{:S(2)}) async-start(), calls=%async_computation.1 | async-start | bytes 294912 | tf_op jit(solution)/shard_map/reduce_scatter | solution.py:138
  330.2 4.6 %collective-permute-start.4 = (bf16[1,3,128,128]{3,2,1,0:T(8,128)(2,1)S(1)}, bf16[1,3,128,128]{3,2,1,0:T(8,128)(2,1)S(1)}, u32[]{:S(2)}, u32[]{:S(2)}) collective-permute-start(bf16[1,3,128,128]{3,2,1,0:T(8,128)(2,1)S(1)} %bitcast.237), channel_id=1, source_target_pairs={{0,8},{8,16},{16,24},{24,32},{32,40},{40,48},{48,56},{56,64},{64,7... | collective-permute-start | bytes 294920 | tf_op jit(solution)/shard_map/ppermute | solution.py:18
  331.5 7.7 %collective-permute-start.5 = (bf16[1,3,128,128]{3,2,1,0:T(8,128)(2,1)S(1)}, bf16[1,3,128,128]{3,2,1,0:T(8,128)(2,1)S(1)}, u32[]{:S(2)}, u32[]{:S(2)}) collective-permute-start(bf16[1,3,128,128]{3,2,1,0:T(8,128)(2,1)S(1)} %bitcast.236), channel_id=1, source_target_pairs={{8,0},{16,8},{24,16},{32,24},{40,32},{48,40},{56,48},{64,56},{72,6... | collective-permute-start | bytes 294920 | tf_op jit(solution)/shard_map/ppermute | solution.py:20
  340.2 3.5 collective-permute-start.6
  341.5 3.3 collective-permute-start.7
Sparse Core Ops, SparseCore 0:
  329.3 79.2 all-reduce.5
  411.0 29.5 reduce-scatter.2
